TPU v7x, 512 devices: a whole 4x8x8 slice. The times are simulated.
512 devices in a mesh: ctx: 32 (over z, x_hi, core), head: 16 (over x_lo, y).
Axes of the slice: x: 4 (x_hi: 2, x_lo: 2; x = x_hi * 2 + x_lo), y: 8, z: 8, core: 2. Of those that a mesh axis runs over, the one named last changes fastest.
Arguments:
- q_nope: bfloat16 [4096, 8192], P('ctx', 'head'), may hold values from -6 to 6
- q_rope: bfloat16 [4096, 4096], P('ctx', 'head'), may hold values from -9 to 9
- latent: bfloat16 [32, 128, 512], P('ctx'), may hold values from -6 to 6
- key_rope: bfloat16 [32, 64, 128], P('ctx'), may hold values from -9 to 9
- chosen: int32 [32, 20], P('ctx'), may hold values from 0 to 31, as said below
- w_uk: bfloat16 [64, 128, 512], P('head'), may hold values from -0.5 to 0.5
- w_uv: bfloat16 [64, 512, 128], P('head'), may hold values from -1.5 to 1.5
- w_out: bfloat16 [8192, 3584], P('head'), may hold values from -0.09375 to 0.09375
Outputs:
- mixed: bfloat16 [4096, 3584], P('ctx', 'head')
Inputs may be any that keep to these rules, and one draw needn't show every extreme that they name: `chosen`: row b lists key blocks numbered 0 to b; b itself always appears, an entry may repeat and then counts once, and row 31 lists 20 different blocks.
All inputs are finite; a program needn't handle non-finite values.
Results may differ from a plain program's by a relative error of at most 0.019.
Values may be sent and summed in bfloat16 or wider, within the bound.
A program may use at most 64 MiB of HBM per device.

v0:
```python
import jax
import jax.numpy as jnp
from jax import lax
from jax.sharding import PartitionSpec as P

LAT = 512
ROPE = 64
QK_NOPE = 128
VHEAD = 128
BLOCK = 128


MASKED_SCORE = -1e30


def absorb(nope_rows, key_up):
    tokens, head_count, feature_count = nope_rows.shape
    grouped = nope_rows.reshape(tokens // BLOCK, BLOCK, head_count, feature_count)
    return jnp.einsum("bihn,hnl->bhil", grouped, key_up, preferred_element_type=jnp.float32).astype(
        jnp.bfloat16
    )


def rope_heads(rope_rows):
    tokens, head_count, feature_count = rope_rows.shape
    return jnp.transpose(
        rope_rows.reshape(tokens // BLOCK, BLOCK, head_count, feature_count), (0, 2, 1, 3)
    )


def attend_block(carried, query_lat, query_rope, lat_block, rope_block, diagonal):
    row_max, row_sum, weighted = carried
    score_scale = (QK_NOPE + ROPE) ** (-0.5)
    scores = jnp.einsum("hil,jl->hij", query_lat, lat_block, preferred_element_type=jnp.float32)
    scores = (
        scores
        + jnp.einsum("hir,rj->hij", query_rope, rope_block, preferred_element_type=jnp.float32)
    ) * score_scale
    row_ids = lax.broadcasted_iota(jnp.int32, (BLOCK, BLOCK), 0)
    col_ids = lax.broadcasted_iota(jnp.int32, (BLOCK, BLOCK), 1)
    allowed = jnp.logical_or(jnp.logical_not(diagonal), col_ids <= row_ids)[None]
    scores = jnp.where(allowed, scores, MASKED_SCORE)
    new_max = jnp.maximum(row_max, jnp.max(scores, axis=-1))
    factor = jnp.exp(row_max - new_max)
    exponent = jnp.where(allowed, jnp.exp(scores - new_max[..., None]), 0.0)
    row_sum = row_sum * factor + jnp.sum(exponent, axis=-1)
    weighted = weighted * factor[..., None] + jnp.einsum(
        "hij,jl->hil", exponent.astype(jnp.bfloat16), lat_block, preferred_element_type=jnp.float32
    )
    return (new_max, row_sum, weighted)


def maybe_attend(selected, carried, query_lat, query_rope, lat_block, rope_block, diagonal):

    def compute(current):
        return attend_block(current, query_lat, query_rope, lat_block, rope_block, diagonal)

    def unchanged(current):
        return current

    return lax.cond(selected, compute, unchanged, carried)


def fresh_state(head_count):
    return (
        jnp.full((head_count, BLOCK), MASKED_SCORE, jnp.float32),
        jnp.zeros((head_count, BLOCK), jnp.float32),
        jnp.zeros((head_count, BLOCK, LAT), jnp.float32),
    )


def finish(carried):
    row_max, row_sum, weighted = carried
    return (weighted / row_sum[..., None]).astype(jnp.bfloat16)


def attend_all(query_lats, query_ropes, key_lists, query_blocks, latent, key_rope):
    query_count = query_lats.shape[0]
    head_count = query_lats.shape[1]
    states = tuple((fresh_state(head_count) for query_id in range(query_count)))
    block_total = latent.shape[0] * lax.axis_size("ctx")
    numbers = jnp.arange(block_total, dtype=jnp.int32)
    wanted = jnp.any(key_lists[:, :, None] == numbers[None, None, :], axis=1)
    lat_piece = lax.all_gather(latent, "ctx", axis=0, tiled=True)
    rope_piece = lax.all_gather(key_rope, "ctx", axis=0, tiled=True)

    def visit_block(current, inputs):
        lat_block, rope_block, offset = inputs
        selected = lax.dynamic_index_in_dim(wanted[0], offset, 0, keepdims=False)
        updated = [
            maybe_attend(
                selected,
                current[0],
                query_lats[0],
                query_ropes[0],
                lat_block,
                rope_block,
                offset == query_blocks[0],
            )
        ]
        return (tuple(updated), None)

    offsets = jnp.arange(lat_piece.shape[0], dtype=jnp.int32)
    finished, unused = lax.scan(visit_block, states, (lat_piece, rope_piece, offsets))
    states = finished
    return jnp.stack([finish(carried) for carried in states], axis=0)


def on_device(q_nope, q_rope, latent, key_rope, chosen, w_uk, w_uv, w_out):
    tokens = q_nope.shape[0]
    head_count = w_uk.shape[0]
    nope_rows = q_nope.reshape(tokens, head_count, QK_NOPE)
    rope_rows = q_rope.reshape(tokens, head_count, ROPE)
    local_blocks = latent.shape[0]
    ctx_place = lax.axis_index("ctx")
    block_offsets = jnp.arange(local_blocks, dtype=jnp.int32)
    own_blocks = ctx_place * local_blocks + block_offsets
    outputs = attend_all(
        absorb(nope_rows, w_uk), rope_heads(rope_rows), chosen, own_blocks, latent, key_rope
    )
    values = jnp.einsum("bhil,hlv->bihv", outputs, w_uv, preferred_element_type=jnp.float32).astype(
        jnp.bfloat16
    )
    value_rows = values.reshape(tokens, head_count * VHEAD)
    partial_sums = jnp.dot(value_rows, w_out, preferred_element_type=jnp.float32)
    return lax.psum_scatter(
        partial_sums.astype(jnp.bfloat16), "head", scatter_dimension=1, tiled=True
    )


def solution(mesh):
    return jax.shard_map(
        on_device,
        mesh=mesh,
        in_specs=(
            P("ctx", "head"),
            P("ctx", "head"),
            P("ctx", None, None),
            P("ctx", None, None),
            P("ctx", None),
            P("head", None, None),
            P("head", None, None),
            P("head", None),
        ),
        out_specs=P("ctx", "head"),
        check_vma=False,
    )
```

profile of v0, /device:TPU:4, one launch (start us, length us, event | category | flops | bytes accessed | tf_op | source)
XLA Modules:
  0.0 388.9 jit_solution(15664699777143357101)
XLA Ops:
  6.5 0.7 all-gather.2.cloned.1.call-update
  7.6 1.3 fusion.23
  9.1 1.0 copy.24
  10.0 0.7 fusion.26
  10.8 45.0 %all_gather.7 = bf16[32,64,128]{2,1,0:T(8,128)(2,1)S(1)} all-gather(bf16[1,64,128]{2,1,0:T(8,128)(2,1)} %param.15), channel_id=1, replica_groups=mesh['ctx'=32,'head'=16] {'ctx'}, dimensions={0}, use_global_device_ids=true | all-gather | bytes 540672 | tf_op jit(solution)/shard_map/all_gather | solution.py:85
  55.8 50.3 %all-gather.2.cloned.1.call-done = bf16[32,128,512]{2,1,0:T(8,128)(2,1)} async-done(((bf16[1,128,512]{2,1,0:T(8,128)(2,1)}), bf16[32,128,512]{2,1,0:T(8,128)(2,1)}) %all-gather.2.cloned.1.call-update) | async-done | bytes 4194320 | tf_op jit(solution)/shard_map/all_gather | solution.py:84
  106.2 130.1 %while.14 = (s32[]{:T(128)}, f32[4,128]{1,0:T(4,128)S(1)}, f32[4,128]{1,0:T(4,128)S(1)}, f32[4,128,512]{2,1,0:T(8,128)S(1)}, s32[32]{0:T(128)S(1)}, /*index=5*/p...) while((s32[]{:T(128)}, f32[4,128]{1,0:T(4,128)S(1)}, ...), condition=%wide.region_6.7_spmd, body=%wide.region_1.6_spmd.sunk | while | flops 143819776 | bytes 4375892 | solution.py:104
  106.2 0.7 dynamic_slice.42
  110.2 0.7 dynamic_slice.42
  114.1 0.7 dynamic_slice.42
  117.4 4.3 %conditional.2 = ((f32[4,128]{1,0:T(4,128)S(1)}, f32[4,128]{1,0:T(4,128)S(1)}, f32[4,128,512]{2,1,0:T(8,128)S(1)})) conditional(s32[]{:T(128)} %bitcast.56, (f32[4,128]{1,0:T(4,128)S(1)}, f32[4,128]{1,0:T(4,128)S(1)}, f32[4,128,512]{2,1,0:T(8,128)S(1)}) %tuple.36, (s32[]{:T(128)}, s32[]{:T(128)}, bf16[32,128,512]{2,1,0:T(8,128)(2,1)}, s32[]{:T(128)}, ...), branch_computations={%region_2.2_spmd, %region_3.5_spmd} | conditional | flops 143819776 | bytes 4375600 | solution.py:61
  119.0 1.2 fusion.27
  120.3 1.4 convolution_add_fusion
  121.7 0.7 dynamic_slice.42
  125.7 0.7 dynamic_slice.42
  129.6 0.7 dynamic_slice.42
  133.6 0.7 dynamic_slice.42
  137.5 0.7 dynamic_slice.42
  141.5 0.7 dynamic_slice.42
  145.4 0.7 dynamic_slice.42
  149.4 0.7 dynamic_slice.42
  153.3 0.7 dynamic_slice.42
  157.3 0.7 dynamic_slice.42
  161.2 0.7 dynamic_slice.42
  165.2 0.7 dynamic_slice.42
  169.1 0.7 dynamic_slice.42
  173.1 0.7 dynamic_slice.42
  177.0 0.7 dynamic_slice.42
  181.0 0.7 dynamic_slice.42
  236.7 1.6 copy-done.1
  238.3 2.5 convolution_convert_fusion
  240.8 141.2 %reduce-scatter.2.cloned.1.call-done = bf16[128,224]{0,1:T(8,128)(2,1)} async-done(((bf16[128,3584]{0,1:T(8,128)(2,1)}), bf16[128,224]{0,1:T(8,128)(2,1)}) %reduce-scatter.2.cloned.1.call-update) | async-done | bytes 57360 | tf_op jit(solution)/shard_map/reduce_scatter | solution.py:126
  (96 shorter events, 48.7 us)
Async XLA Ops:
  6.5 1.0 copy-start
  6.5 99.5 %all-gather.2.cloned.1.call-start = ((), (), s32[]{:S(2)}) async-start(), calls=%async_computation.1 | async-start | bytes 4325376 | tf_op jit(solution)/shard_map/all_gather | solution.py:84
  7.3 374.8 %reduce-scatter.2.cloned.1.call-start = ((), (), s32[]{:S(2)}) async-start(), calls=%async_computation.2 | async-start | bytes 974848 | tf_op jit(solution)/shard_map/reduce_scatter | solution.py:126
  106.2 130.1 %copy-start.2 = (bf16[4,512,128]{2,1,0:T(8,128)(2,1)S(1)}, bf16[4,512,128]{2,1,0:T(8,128)(2,1)}, u32[]{:S(2)}) copy-start(bf16[4,512,128]{2,1,0:T(8,128)(2,1)} %param.18) | copy-start | bytes 1572868
  236.3 2.0 copy-start.1
Sparse Core Ops, SparseCore 0:
  10.7 95.2 all-gather.1
  241.0 141.0 reduce-scatter.1
where the time goes:
time: 392 us; the launch traced here: 389 us
  waiting for transfers between devices  192 us (49%)
  loops' own time  86.5 us (22%)
  blocking collectives  45 us (11%)
  local copies, waits for them, and re-layouts  24 us (6%)
  other arithmetic  20.6 us (5%)
  between operations  13.5 us (3%)
  matrix products  7.02 us (2%)
    reduce_scatter x1, waiting for transfers between devices, on_device(): lax.psum_scatter(partial_sums.astype(jnp.bfloat16), 'head', scatter_dimen...  141 us
    another operation x1, loops' own time, attend_all(): lax.scan(visit_block, states, (lat_piece, rope_piece, offsets))  66.1 us
    all_gather x1, waiting for transfers between devices, attend_all(): lat_piece = lax.all_gather(latent, 'ctx', axis=0, tiled=True)  50.3 us
    all_gather x1, blocking collectives, attend_all(): rope_piece = lax.all_gather(key_rope, 'ctx', axis=0, tiled=True)  45 us
    dynamic_slice x32, local copies, waits for them, and re-layouts, attend_all(): lax.scan(visit_block, states, (lat_piece, rope_piece, offsets))  20.9 us
    another operation x32, loops' own time, maybe_attend(): return lax.cond(selected, compute, unchanged, carried)  20.5 us
    convert_element_type x32, other arithmetic, maybe_attend(): return lax.cond(selected, compute, unchanged, carried)  19.7 us
  transfers between devices with their start and end apart: 2, of which 2 were waited for; matrix products, arithmetic and copies ran while one was open for 1% of the time, Pallas kernels for 0%

commit v1 on v0

v1 whole, which is shorter than its diff:
```python
import math

import jax
import jax.numpy as jnp
from jax import lax
from jax.experimental import pallas as pl
from jax.experimental.pallas import tpu as pltpu
from jax.sharding import PartitionSpec as P

LAT = 512
ROPE = 64
QK_NOPE = 128
VHEAD = 128
BLOCK = 128
ROWS = 144
THIRD = 48
PIECES = 3
MASKED = -1e30
MESH = pl.DeviceIdType.MESH


def gather_attend(
    heads,
    planes,
    ys,
    q_nope,
    q_rope,
    latent,
    key_rope,
    chosen,
    w_uk,
    w_uv,
    values,
    kv,
    qn_buf,
    qr_buf,
    wuk_buf,
    wuv_buf,
    q_lat,
    q_rot,
    bias,
    row_max,
    row_sum,
    acc,
    load_sem,
    x_send,
    x_recv,
    own_send,
    own_recv,
    xp_send,
    xp_recv,
    z_send,
    z_recv,
    y_send,
    y_recv,
    zp_send,
    zp_recv,
    yp_send,
    yp_recv,
):
    ci = lax.axis_index("ctx")
    hi = lax.axis_index("head")
    z, xh, core = ci // 4, (ci // 2) % 2, ci % 2
    xl, y = hi // ys, hi % ys
    color = y % 2

    def ctx_at(zz):
        return lax.rem(zz + planes, planes) * 4 + xh * 2 + core

    def head_at(yy):
        return xl * ys + lax.rem(yy + ys, ys)

    partner = (z * 4 + xh * 2 + (1 - core), hi)
    across = (z * 4 + (1 - xh) * 2 + core, (1 - xl) * ys + y)
    z_next, z_prev = (ctx_at(z + 1), hi), (ctx_at(z - 1), hi)
    y_next, y_prev = (ci, head_at(y + 1)), (ci, head_at(y - 1))
    toward_z = (z_next, z_prev)
    toward_y = (y_next, y_prev)

    loads = [pltpu.make_async_copy(latent.at[0], kv.at[ci, 0:BLOCK, :], load_sem.at[0])]
    for i in range(4):
        loads.append(
            pltpu.make_async_copy(
                key_rope.at[0, 16 * i : 16 * i + 16, :],
                kv.at[ci, BLOCK:ROWS, 128 * i : 128 * i + 128],
                load_sem.at[1 + i],
            )
        )
    for i, (src, dst) in enumerate(
        ((q_nope, qn_buf), (w_uk, wuk_buf), (q_rope, qr_buf), (w_uv, wuv_buf))
    ):
        loads.append(pltpu.make_async_copy(src, dst, load_sem.at[5 + i]))
    for copy in loads:
        copy.start()

    barrier = pltpu.get_barrier_semaphore()
    for device in (partner, across, z_next, z_prev, y_next, y_prev):
        pl.semaphore_signal(barrier, inc=1, device_id=device, device_id_type=MESH)
    pl.semaphore_wait(barrier, 6)

    def part(block, p):
        return kv.at[block, THIRD * p : THIRD * (p + 1), :]

    def send(block, p, send_sem, recv_sem, device):
        return pltpu.make_async_remote_copy(
            part(block, p), part(block, p), send_sem, recv_sem, device_id=device, device_id_type=MESH
        )

    def plane_of(d, hop):
        return lax.rem(z + planes - hop, planes) if d == 0 else lax.rem(z + hop, planes)

    def mine(plane):
        return plane * 4 + color * 2 + core

    def other(plane):
        return plane * 4 + (1 - color) * 2 + core

    def z_copy(d, hop, p):
        return send(mine(plane_of(d, hop - 1)), p, z_send.at[d, hop - 1, p], z_recv.at[d, hop - 1, p], toward_z[d])

    def y_copy(d, hop, p):
        return send(mine(plane_of(d, hop)), p, y_send.at[d, hop - 1, p], y_recv.at[d, hop - 1, p], toward_y[d])

    def y_arrival(d, hop, p):
        return send(other(plane_of(d, hop)), p, y_send.at[d, hop - 1, p], y_recv.at[d, hop - 1, p], toward_y[d])

    def zp_copy(d, hop, p):
        return send(mine(plane_of(d, hop)), p, zp_send.at[d, hop - 1, p], zp_recv.at[d, hop - 1, p], partner)

    def yp_copy(d, hop, p):
        return send(other(plane_of(d, hop)), p, yp_send.at[d, hop - 1, p], yp_recv.at[d, hop - 1, p], partner)

    def carried(d, hop, p):
        return hop < 4 or (p < 2 if d == 0 else p == 2)

    for copy in loads[:5]:
        copy.wait()
    across_block = z * 4 + (1 - xh) * 2 + core
    x_copies = [send(ci, p, x_send.at[p], x_recv.at[p], across) for p in range(PIECES)]
    for copy in x_copies:
        copy.start()
    own_copy = pltpu.make_async_remote_copy(
        kv.at[ci], kv.at[ci], own_send.at[0], own_recv.at[0], device_id=partner, device_id_type=MESH
    )
    own_copy.start()

    @pl.when(xh == color)
    def _():
        for p in range(PIECES):
            for d in range(2):
                z_copy(d, 1, p).start()

    block_ids = lax.broadcasted_iota(jnp.int32, (planes * 4, BLOCK), 0)
    listed = block_ids < 0
    for j in range(chosen.shape[1]):
        listed = jnp.logical_or(listed, block_ids == chosen[0, j])
    bias[...] = jnp.where(listed, 0.0, MASKED)
    row_max[...] = jnp.full_like(row_max, MASKED)
    row_sum[...] = jnp.zeros_like(row_sum)
    acc[...] = jnp.zeros_like(acc)

    xp_copies = [send(across_block, p, xp_send.at[p], xp_recv.at[p], partner) for p in range(PIECES)]
    for p in range(PIECES):
        x_copies[p].wait_recv()
        xp_copies[p].start()

        @pl.when(xh != color)
        def _():
            for d in range(2):
                z_copy(d, 1, p).start()

    for copy in loads[5:8]:
        copy.wait()
    for h in range(heads):
        rows = slice(BLOCK * h, BLOCK * (h + 1))
        q_lat[rows, :] = jnp.dot(
            qn_buf[:, QK_NOPE * h : QK_NOPE * (h + 1)], wuk_buf[h], preferred_element_type=jnp.float32
        ).astype(jnp.bfloat16)
        q_rot[rows, :] = qr_buf[:, ROPE * h : ROPE * (h + 1)]

    scale = (QK_NOPE + ROPE) ** -0.5 * math.log2(math.e)
    half = heads * BLOCK // 2

    def attend(plane, r, own):
        rows = slice(half * r, half * (r + 1))
        first = plane * 4
        keys = jnp.concatenate([kv[first + i, 0:BLOCK, :] for i in range(4)], axis=0)
        rotary = jnp.concatenate(
            [
                jnp.concatenate(
                    [kv[first + i, BLOCK:ROWS, 128 * j : 128 * (j + 1)] for j in range(4)], axis=0
                )
                for i in range(4)
            ],
            axis=1,
        )
        scores = lax.dot_general(
            q_lat[rows, :], keys, (((1,), (1,)), ((), ())), preferred_element_type=jnp.float32
        )
        scores = scores + jnp.dot(q_rot[rows, :], rotary, preferred_element_type=jnp.float32)
        hidden = jnp.concatenate([bias[pl.ds(first + i, 1), :] for i in range(4)], axis=1)
        scores = scores * scale + hidden
        if own:
            t_ids = lax.broadcasted_iota(jnp.int32, scores.shape, 0) % BLOCK
            col_ids = lax.broadcasted_iota(jnp.int32, scores.shape, 1)
            u_ids = col_ids - (ci % 4) * BLOCK
            later = (u_ids > t_ids) & (u_ids < BLOCK)
            scores = jnp.where(later, MASKED, scores)
        old_max = row_max[rows, :]
        new_max = jnp.maximum(old_max, jnp.max(scores, axis=1, keepdims=True))
        factor = jnp.exp2(old_max - new_max)
        wide = jnp.concatenate([new_max] * 4, axis=1)
        exponent = jnp.exp2(scores - wide)
        total = exponent[:, 0:128] + exponent[:, 128:256] + exponent[:, 256:384] + exponent[:, 384:512]
        row_max[rows, :] = new_max
        row_sum[rows, :] = row_sum[rows, :] * factor + total
        acc[rows, :] = acc[rows, :] * jnp.concatenate([factor] * 4, axis=1) + jnp.dot(
            exponent.astype(jnp.bfloat16), keys, preferred_element_type=jnp.float32
        )

    def z_arrive(d, hop, p):
        z_copy(d, hop, p).wait_recv()

    own_copy.wait_recv()
    for p in range(PIECES):
        xp_copies[p].wait_recv()

    def step(hop, c):
        for p in range(PIECES):
            for d in range(2):

                @pl.when((hop < 4) | ((hop == 4) & (p < 2 if d == 0 else p == 2)))
                def _():
                    z_copy(d, hop, p).wait_recv()

                @pl.when((hop < 3) | ((hop == 3) & (p < 2 if d == 0 else p == 2)))
                def _():
                    z_copy(d, hop + 1, p).start()

                @pl.when((hop < 4) | ((hop == 4) & (p < 2 if d == 0 else p == 2)))
                def _():
                    y_copy(d, hop, p).start()
                    zp_copy(d, hop, p).start()

            before = hop - 1
            for d in range(2):

                @pl.when((before >= 1) & ((before < 4) | ((before == 4) & (p < 2 if d == 0 else p == 2))))
                def _():
                    y_arrival(d, before, p).wait_recv()
                    yp_copy(d, before, p).start()

            if p == 0:

                @pl.when(hop == 1)
                def _():
                    for r in range(2):
                        attend(z, r, True)

            ready = hop - 2
            if p > 0:
                d = p - 1

                @pl.when((ready >= 1) & (ready < 4))
                def _():
                    for q in range(PIECES):
                        zp_copy(d, ready, q).wait_recv()
                        yp_copy(d, ready, q).wait_recv()
                    for r in range(2):
                        attend(plane_of(d, ready), r, False)

        return c

    lax.fori_loop(1, 6, step, 0)
    for d in range(2):
        for p in range(PIECES):
            if carried(d, 4, p):
                zp_copy(d, 4, p).wait_recv()
                yp_copy(d, 4, p).wait_recv()
    for r in range(2):
        attend(plane_of(0, 4), r, False)

    loads[8].wait()
    for h in range(heads):
        rows = slice(BLOCK * h, BLOCK * (h + 1))
        denominator = jnp.sum(row_sum[rows, :], axis=1, keepdims=True)
        mix = (acc[rows, :] / denominator).astype(jnp.bfloat16)
        values[:, VHEAD * h : VHEAD * (h + 1)] = jnp.dot(
            mix, wuv_buf[h], preferred_element_type=jnp.float32
        ).astype(jnp.bfloat16)

    for copy in x_copies + xp_copies + [own_copy]:
        copy.wait_send()
    for d in range(2):
        for hop in range(1, 5):
            for p in range(PIECES):
                if carried(d, hop, p):
                    z_copy(d, hop, p).wait_send()
                    y_copy(d, hop, p).wait_send()
                    zp_copy(d, hop, p).wait_send()
                    yp_copy(d, hop, p).wait_send()


def solution(mesh):
    planes = mesh.shape["ctx"] // 4
    ys = mesh.shape["head"] // 2

    def on_device(q_nope, q_rope, latent, key_rope, chosen, w_uk, w_uv, w_out):
        heads = w_uk.shape[0]
        tokens = q_nope.shape[0]
        rows = heads * tokens
        anywhere = pl.BlockSpec(memory_space=pl.ANY)
        dma = pltpu.SemaphoreType.DMA

        def kernel(*refs):
            gather_attend(heads, planes, ys, *refs)

        values = pl.pallas_call(
            kernel,
            out_shape=jax.ShapeDtypeStruct((tokens, heads * VHEAD), jnp.bfloat16),
            in_specs=[
                anywhere,
                anywhere,
                anywhere,
                anywhere,
                pl.BlockSpec(memory_space=pltpu.SMEM),
                anywhere,
                anywhere,
            ],
            out_specs=pl.BlockSpec(memory_space=pltpu.VMEM),
            scratch_shapes=[
                pltpu.VMEM((planes * 4, ROWS, LAT), jnp.bfloat16),
                pltpu.VMEM(q_nope.shape, jnp.bfloat16),
                pltpu.VMEM(q_rope.shape, jnp.bfloat16),
                pltpu.VMEM(w_uk.shape, jnp.bfloat16),
                pltpu.VMEM(w_uv.shape, jnp.bfloat16),
                pltpu.VMEM((rows, LAT), jnp.bfloat16),
                pltpu.VMEM((rows, ROPE), jnp.bfloat16),
                pltpu.VMEM((planes * 4, BLOCK), jnp.float32),
                pltpu.VMEM((rows, 128), jnp.float32),
                pltpu.VMEM((rows, 128), jnp.float32),
                pltpu.VMEM((rows, LAT), jnp.float32),
                dma((9,)),
                dma((3,)),
                dma((3,)),
                dma((1,)),
                dma((1,)),
                dma((3,)),
                dma((3,)),
            ]
            + [dma((2, 4, 3))] * 8,
            compiler_params=pltpu.CompilerParams(
                collective_id=0, has_side_effects=True, vmem_limit_bytes=48 << 20
            ),
        )(q_nope, q_rope, latent, key_rope, chosen, w_uk, w_uv)
        partial = jnp.dot(values, w_out, preferred_element_type=jnp.float32)
        return lax.psum_scatter(
            partial.astype(jnp.bfloat16), "head", scatter_dimension=1, tiled=True
        )

    return jax.shard_map(
        on_device,
        mesh=mesh,
        in_specs=(
            P("ctx", "head"),
            P("ctx", "head"),
            P("ctx", None, None),
            P("ctx", None, None),
            P("ctx", None),
            P("head", None, None),
            P("head", None, None),
            P("head", None),
        ),
        out_specs=P("ctx", "head"),
        check_vma=False,
    )
```

time: 392 us -> 136 us (0.35)
  waiting for transfers between devices: 192 us -> 70.8 us
  loops' own time: 86.5 us -> 0 us
  blocking collectives: 45 us -> 0 us
  Pallas kernels: 0 us -> 41 us
  other arithmetic: 20.6 us -> 0 us
  local copies, waits for them, and re-layouts: 24 us -> 6.1 us
    another operation x33 -> x0, loops' own time: 86.5 us -> none  [the longest x1 66.1 us: attend_all(): lax.scan(visit_block, states, (lat_piece, rope_piece, offsets))]
    reduce_scatter x1, waiting for transfers between devices: 141 us -> 70.8 us  [on_device(): lax.psum_scatter(partial.astype(jnp.bfloat16), 'head', scatter_dimension=...]
    all_gather x1 -> x0, waiting for transfers between devices: 50.3 us -> none  [attend_all(): lat_piece = lax.all_gather(latent, 'ctx', axis=0, tiled=True)]
    all_gather x1 -> x0, blocking collectives: 45 us -> none  [attend_all(): rope_piece = lax.all_gather(key_rope, 'ctx', axis=0, tiled=True)]
    pallas_call x0 -> x1, Pallas kernels: none -> 41 us  [on_device(): pl.pallas_call(kernel, out_shape=jax.ShapeDtypeStruct((tokens, heads * VH...]
    dynamic_slice x32 -> x0, local copies, waits for them, and re-layouts: 20.9 us -> none  [attend_all(): lax.scan(visit_block, states, (lat_piece, rope_piece, offsets))]
    convert_element_type x32 -> x0, other arithmetic: 19.7 us -> none  [maybe_attend(): return lax.cond(selected, compute, unchanged, carried)]
  transfers between devices with their start and end apart: 2 -> 1, of which waited for: 2 -> 1; matrix products, arithmetic and copies ran while one was open for 1% -> 0% of each run, Pallas kernels for 0% -> 0%
where the time goes in v1:
time: 136 us
  waiting for transfers between devices  70.8 us (52%)
  Pallas kernels  41 us (30%)
  between operations  13.4 us (10%)
  local copies, waits for them, and re-layouts  6.1 us (4%)
  matrix products  4.53 us (3%)
    reduce_scatter x1, waiting for transfers between devices, on_device(): lax.psum_scatter(partial.astype(jnp.bfloat16), 'head', scatter_dimension=...  70.8 us
    pallas_call x1, Pallas kernels, on_device(): pl.pallas_call(kernel, out_shape=jax.ShapeDtypeStruct((tokens, heads * VH...  41 us
    unnamed x14, local copies, waits for them, and re-layouts  6.1 us
    dot_general x1, matrix products, on_device(): partial = jnp.dot(values, w_out, preferred_element_type=jnp.float32)  4.53 us
  transfers between devices with their start and end apart: 1, of which 1 were waited for; matrix products, arithmetic and copies ran while one was open for 0% of the time, Pallas kernels for 0%

profile of v1, /device:TPU:4, one launch (start us, length us, event | category | flops | bytes accessed | tf_op | source)
XLA Modules:
  0.0 135.8 jit_solution(841588775927341853)
XLA Ops:
  6.5 0.0 reduce-scatter.2.cloned.1.call-start
  6.5 0.0 copy-start
  6.5 1.0 copy-done
  7.6 0.0 copy-start.1
  7.6 1.0 copy-done.1
  8.6 0.0 copy-start.2
  8.6 0.9 copy-done.2
  9.5 0.0 copy-start.3
  9.5 0.9 copy-done.3
  10.4 0.0 copy-start.4
  10.4 0.8 copy-done.4
  11.3 0.0 copy-start.5
  11.3 0.7 copy-done.5
  12.0 0.0 copy-start.6
  12.0 0.7 copy-done.6
  12.6 41.0 %shard_map.82 = bf16[128,512]{1,0:T(8,128)(2,1)S(1)} custom-call(bf16[128,512]{1,0:T(8,128)(2,1)S(1)} %copy-done.2, bf16[128,256]{1,0:T(8,128)(2,1)S(1)} %copy-done.4, bf16[1,128,512]{2,1,0:T(8,128)(2,1)S(1)} %copy-done.3, bf16[1,64,128]{2,1,0:T(8,128)(2,1)S(1)} %copy-done.5, s32[1,20]{1,0:T(1,128)S(1)} %copy-done.6, bf16[4,128,512]{2,1,0:T(8,128)(2,1)S(1)} %copy-done, ...), custom_call_target="tpu_custom_call" | custom-call | tf_op jit(solution)/shard_map/pallas_call | solution.py:318
  53.6 4.5 %convolution_convert_fusion = bf16[128,3584]{0,1:T(8,128)(2,1)} fusion(bf16[128,512]{1,0:T(8,128)(2,1)S(1)} %shard_map.82, bf16[512,3584]{1,0:T(8,128)(2,1)} %param.15), kind=kOutput, calls=%fused_computation | convolution fusion | flops 470220800 | bytes 4718592 | tf_op jit(solution)/shard_map/dot_general | solution.py:356
  58.2 0.0 reduce-scatter.2.cloned.1.call-update
  58.2 70.8 %reduce-scatter.2.cloned.1.call-done = bf16[128,224]{0,1:T(8,128)(2,1)} async-done(((bf16[128,3584]{0,1:T(8,128)(2,1)}), bf16[128,224]{0,1:T(8,128)(2,1)}) %reduce-scatter.2.cloned.1.call-update) | async-done | bytes 57360 | tf_op jit(solution)/shard_map/reduce_scatter | solution.py:357
Async XLA Ops:
  6.5 122.4 %reduce-scatter.2.cloned.1.call-start = ((), (), s32[]{:S(2)}) async-start(), calls=%async_computation.1 | async-start | bytes 974848 | tf_op jit(solution)/shard_map/reduce_scatter | solution.py:357
  6.5 1.0 copy-start
  7.6 1.0 copy-start.1
  8.6 0.9 copy-start.2
  9.5 0.9 copy-start.3
  10.4 0.8 copy-start.4
  11.3 0.7 copy-start.5
  12.0 0.7 copy-start.6
Sparse Core Ops, SparseCore 0:
  58.3 70.5 reduce-scatter.1

commit v2 on v1

--- a/solution.py
+++ b/solution.py
@@ -30,7 +30,8 @@
     chosen,
     w_uk,
     w_uv,
-    values,
+    w_out,
+    out,
     kv,
     qn_buf,
     qr_buf,
@@ -57,6 +58,20 @@
     zp_recv,
     yp_send,
     yp_recv,
+    w_mine,
+    w_peer,
+    w_turned,
+    values,
+    v_peer,
+    piece,
+    staged,
+    landed,
+    w_send,
+    w_recv,
+    v_send,
+    v_recv,
+    r_send,
+    r_recv,
 ):
     ci = lax.axis_index("ctx")
     hi = lax.axis_index("head")
@@ -72,6 +87,7 @@
 
     partner = (z * 4 + xh * 2 + (1 - core), hi)
     across = (z * 4 + (1 - xh) * 2 + core, (1 - xl) * ys + y)
+    beside = (ci, (1 - xl) * ys + y)
     z_next, z_prev = (ctx_at(z + 1), hi), (ctx_at(z - 1), hi)
     y_next, y_prev = (ci, head_at(y + 1)), (ci, head_at(y - 1))
     toward_z = (z_next, z_prev)
@@ -90,13 +106,19 @@
         ((q_nope, qn_buf), (w_uk, wuk_buf), (q_rope, qr_buf), (w_uv, wuv_buf))
     ):
         loads.append(pltpu.make_async_copy(src, dst, load_sem.at[5 + i]))
+    width = w_mine.shape[1]
+    cut = out.shape[0]
+    quarter = w_mine.shape[0] // 4
+    my_columns = pl.ds(pl.multiple_of(xl * width, width), width)
+    peer_columns = pl.ds(pl.multiple_of((1 - xl) * width, width), width)
+    loads.append(pltpu.make_async_copy(w_out.at[:, my_columns], w_mine, load_sem.at[9]))
     for copy in loads:
         copy.start()
 
     barrier = pltpu.get_barrier_semaphore()
-    for device in (partner, across, z_next, z_prev, y_next, y_prev):
+    for device in (partner, across, beside, z_next, z_prev, y_next, y_prev):
         pl.semaphore_signal(barrier, inc=1, device_id=device, device_id_type=MESH)
-    pl.semaphore_wait(barrier, 6)
+    pl.semaphore_wait(barrier, 7)
 
     def part(block, p):
         return kv.at[block, THIRD * p : THIRD * (p + 1), :]
@@ -149,6 +171,34 @@
         for p in range(PIECES):
             for d in range(2):
                 z_copy(d, 1, p).start()
+
+    def w_rows(which, of_core):
+        return pl.ds(pl.multiple_of((2 * of_core + which) * quarter, quarter), quarter)
+
+    w_copies = [
+        pltpu.make_async_remote_copy(
+            w_out.at[w_rows(which, core), peer_columns],
+            w_peer.at[w_rows(which, core), :],
+            w_send.at[which],
+            w_recv.at[which],
+            device_id=device,
+            device_id_type=MESH,
+        )
+        for which, device in enumerate((beside, across))
+    ]
+    wp_copies = [
+        pltpu.make_async_remote_copy(
+            w_peer.at[w_rows(which, core), :],
+            w_peer.at[w_rows(which, core), :],
+            w_send.at[2 + which],
+            w_recv.at[2 + which],
+            device_id=partner,
+            device_id_type=MESH,
+        )
+        for which in range(2)
+    ]
+    for copy in w_copies:
+        copy.start()
 
     block_ids = lax.broadcasted_iota(jnp.int32, (planes * 4, BLOCK), 0)
     listed = block_ids < 0
@@ -218,8 +268,10 @@
             exponent.astype(jnp.bfloat16), keys, preferred_element_type=jnp.float32
         )
 
-    def z_arrive(d, hop, p):
-        z_copy(d, hop, p).wait_recv()
+    def turn(source, which):
+        for j in range(width // 128):
+            columns = slice(128 * j, 128 * (j + 1))
+            w_turned[which, columns, :] = source[:, columns].T
 
     own_copy.wait_recv()
     for p in range(PIECES):
@@ -256,6 +308,26 @@
                 def _():
                     for r in range(2):
                         attend(z, r, True)
+
+            if p == 2:
+
+                @pl.when(hop == 1)
+                def _():
+                    loads[9].wait()
+                    turn(w_mine, 0)
+
+                @pl.when(hop == 4)
+                def _():
+                    for copy in w_copies:
+                        copy.wait_recv()
+                    for copy in wp_copies:
+                        copy.start()
+
+                @pl.when(hop == 5)
+                def _():
+                    for copy in wp_copies:
+                        copy.wait_recv()
+                    turn(w_peer, 1)
 
             ready = hop - 2
             if p > 0:
@@ -281,14 +353,103 @@
         attend(plane_of(0, 4), r, False)
 
     loads[8].wait()
+    v_copies = []
     for h in range(heads):
         rows = slice(BLOCK * h, BLOCK * (h + 1))
+        columns = slice(VHEAD * h, VHEAD * (h + 1))
         denominator = jnp.sum(row_sum[rows, :], axis=1, keepdims=True)
         mix = (acc[rows, :] / denominator).astype(jnp.bfloat16)
-        values[:, VHEAD * h : VHEAD * (h + 1)] = jnp.dot(
-            mix, wuv_buf[h], preferred_element_type=jnp.float32
-        ).astype(jnp.bfloat16)
-
+        values[:, columns] = jnp.dot(mix, wuv_buf[h], preferred_element_type=jnp.float32).astype(jnp.bfloat16)
+        v_copies.append(
+            pltpu.make_async_remote_copy(
+                values.at[:, columns],
+                v_peer.at[:, columns],
+                v_send.at[h],
+                v_recv.at[h],
+                device_id=beside,
+                device_id_type=MESH,
+            )
+        )
+        v_copies[h].start()
+
+    def owner(step):
+        return lax.rem(y + step + 2 * ys, ys)
+
+    def product(step, which, features):
+        rows = pl.ds(pl.multiple_of(owner(step) * cut, 16), cut)
+        return lax.dot_general(
+            w_turned[which, rows, :],
+            features[...],
+            (((1,), (1,)), ((), ())),
+            preferred_element_type=jnp.float32,
+        )
+
+    def own_part(step):
+        piece[owner(step)] = product(step, 0, values)
+
+    def peer_part(step):
+        piece[owner(step)] += product(step, 1, v_peer)
+
+    steps = [4, 3, -3, 2, -2, 1, -1, 0]
+    for step_at in steps:
+        own_part(step_at)
+    for copy in v_copies:
+        copy.wait_recv()
+
+    rows_half = piece.shape[1] // 2
+
+    def hops_of(d, t):
+        return 4 if (d == 0) == (t == 0) else 3
+
+    def r_copy(d, t, k):
+        return pltpu.make_async_remote_copy(
+            staged.at[d, t, k - 1],
+            landed.at[d, t, k - 1],
+            r_send.at[d, t, k - 1],
+            r_recv.at[d, t, k - 1],
+            device_id=toward_y[d],
+            device_id_type=MESH,
+        )
+
+    def my_rows(step, t):
+        return piece[owner(step), rows_half * t : rows_half * (t + 1), :]
+
+    def send_sum(d, t, k):
+        away = hops_of(d, t) - k + 1
+        total = my_rows(away if d == 0 else -away, t)
+        if k > 1:
+            r_copy(d, t, k - 1).wait_recv()
+            total = total + landed[d, t, k - 2].astype(jnp.float32)
+        staged[d, t, k - 1] = total.astype(jnp.bfloat16)
+        r_copy(d, t, k).start()
+
+    chains = [(0, 0), (1, 1), (0, 1), (1, 0)]
+    peer_part(4)
+    send_sum(0, 0, 1)
+    send_sum(1, 1, 1)
+    peer_part(3)
+    send_sum(0, 1, 1)
+    peer_part(-3)
+    send_sum(1, 0, 1)
+    for step_at in (2, -2, 1, -1, 0):
+        peer_part(step_at)
+    for k in range(2, 5):
+        for d, t in chains:
+            if k <= hops_of(d, t):
+                send_sum(d, t, k)
+    for t in (1, 0):
+        total = my_rows(0, t)
+        for d in range(2):
+            n = hops_of(d, t)
+            r_copy(d, t, n).wait_recv()
+            total = total + landed[d, t, n - 1].astype(jnp.float32)
+        out[rows_half * t : rows_half * (t + 1), :] = total.astype(jnp.bfloat16)
+
+    for d, t in chains:
+        for k in range(1, hops_of(d, t) + 1):
+            r_copy(d, t, k).wait_send()
+    for copy in w_copies + wp_copies + v_copies:
+        copy.wait_send()
     for copy in x_copies + xp_copies + [own_copy]:
         copy.wait_send()
     for d in range(2):
@@ -315,15 +476,19 @@
         def kernel(*refs):
             gather_attend(heads, planes, ys, *refs)
 
-        values = pl.pallas_call(
+        depth = heads * VHEAD
+        width = w_out.shape[1] // 2
+        cut = width // ys
+        return pl.pallas_call(
             kernel,
-            out_shape=jax.ShapeDtypeStruct((tokens, heads * VHEAD), jnp.bfloat16),
+            out_shape=jax.ShapeDtypeStruct((cut, tokens), jnp.bfloat16),
             in_specs=[
                 anywhere,
                 anywhere,
                 anywhere,
                 anywhere,
                 pl.BlockSpec(memory_space=pltpu.SMEM),
+                anywhere,
                 anywhere,
                 anywhere,
             ],
@@ -340,7 +505,7 @@
                 pltpu.VMEM((rows, 128), jnp.float32),
                 pltpu.VMEM((rows, 128), jnp.float32),
                 pltpu.VMEM((rows, LAT), jnp.float32),
-                dma((9,)),
+                dma((10,)),
                 dma((3,)),
                 dma((3,)),
                 dma((1,)),
@@ -348,15 +513,27 @@
                 dma((3,)),
                 dma((3,)),
             ]
-            + [dma((2, 4, 3))] * 8,
+            + [dma((2, 4, 3))] * 8
+            + [
+                pltpu.VMEM((depth, width), jnp.bfloat16),
+                pltpu.VMEM((depth, width), jnp.bfloat16),
+                pltpu.VMEM((2, width, depth), jnp.bfloat16),
+                pltpu.VMEM((tokens, depth), jnp.bfloat16),
+                pltpu.VMEM((tokens, depth), jnp.bfloat16),
+                pltpu.VMEM((ys, cut, tokens), jnp.float32),
+                pltpu.VMEM((2, 2, 4, cut // 2, tokens), jnp.bfloat16),
+                pltpu.VMEM((2, 2, 4, cut // 2, tokens), jnp.bfloat16),
+                dma((4,)),
+                dma((4,)),
+                dma((heads,)),
+                dma((heads,)),
+                dma((2, 2, 4)),
+                dma((2, 2, 4)),
+            ],
             compiler_params=pltpu.CompilerParams(
-                collective_id=0, has_side_effects=True, vmem_limit_bytes=48 << 20
+                collective_id=0, has_side_effects=True, vmem_limit_bytes=67043328
             ),
-        )(q_nope, q_rope, latent, key_rope, chosen, w_uk, w_uv)
-        partial = jnp.dot(values, w_out, preferred_element_type=jnp.float32)
-        return lax.psum_scatter(
-            partial.astype(jnp.bfloat16), "head", scatter_dimension=1, tiled=True
-        )
+        )(q_nope, q_rope, latent, key_rope, chosen, w_uk, w_uv, w_out).T
 
     return jax.shard_map(
         on_device,

time: 136 us -> 63.3 us (0.47)
  the two profiles are of different devices: /device:TPU:4 before, /device:TPU:10 now
where the time goes in v2:
time: 63.3 us; the launch traced here: 63.2 us
  Pallas kernels  61.7 us (97%)
  local copies, waits for them, and re-layouts  1.45 us (2%)
    pallas_call x1, Pallas kernels, on_device(): pl.pallas_call(kernel, out_shape=jax.ShapeDtypeStruct((cut, tokens), jnp....  61.7 us
    unnamed x1, local copies, waits for them, and re-layouts  1.45 us

profile of v2, /device:TPU:10, one launch (start us, length us, event | category | flops | bytes accessed | tf_op | source)
XLA Modules:
  0.0 63.2 jit_solution(12193911527617788035)
XLA Ops:
  0.0 61.7 %shard_map.82 = bf16[224,128]{1,0:T(8,128)(2,1)} custom-call(bf16[128,512]{1,0:T(8,128)(2,1)} %refs_0_.1, bf16[128,256]{1,0:T(8,128)(2,1)} %refs_1_.1, bf16[1,128,512]{2,1,0:T(8,128)(2,1)} %refs_2_.1, bf16[1,64,128]{2,1,0:T(8,128)(2,1)} %refs_3_.1, s32[1,20]{1,0:T(1,128)} %refs_4_.1, bf16[4,128,512]{2,1,0:T(8,128)(2,1)} %refs_5_.1, ...), custom_call_target="tpu_custom_call" | custom-call | tf_op jit(solution)/shard_map/pallas_call | solution.py:482
  61.7 1.4 %copy.10 = bf16[128,224]{0,1:T(8,128)(2,1)} copy(bf16[128,224]{0,1:T(8,128)(2,1)} %bitcast.1) | data formatting | bytes 114688

commit v3 on v2

--- a/solution.py
+++ b/solution.py
@@ -27,7 +27,7 @@
     q_rope,
     latent,
     key_rope,
-    chosen,
+    chosen_hbm,
     w_uk,
     w_uv,
     w_out,
@@ -72,6 +72,7 @@
     v_recv,
     r_send,
     r_recv,
+    chosen,
 ):
     ci = lax.axis_index("ctx")
     hi = lax.axis_index("head")
@@ -90,8 +91,10 @@
     beside = (ci, (1 - xl) * ys + y)
     z_next, z_prev = (ctx_at(z + 1), hi), (ctx_at(z - 1), hi)
     y_next, y_prev = (ci, head_at(y + 1)), (ci, head_at(y - 1))
-    toward_z = (z_next, z_prev)
-    toward_y = (y_next, y_prev)
+    z_over, z_under = (ctx_at(z + 2), hi), (ctx_at(z - 2), hi)
+    y_over, y_under = (ci, head_at(y + 2)), (ci, head_at(y - 2))
+    toward_z = ((z_next, z_prev), (z_over, z_under))
+    toward_y = ((y_next, y_prev), (y_over, y_under))
 
     loads = [pltpu.make_async_copy(latent.at[0], kv.at[ci, 0:BLOCK, :], load_sem.at[0])]
     for i in range(4):
@@ -112,13 +115,15 @@
     my_columns = pl.ds(pl.multiple_of(xl * width, width), width)
     peer_columns = pl.ds(pl.multiple_of((1 - xl) * width, width), width)
     loads.append(pltpu.make_async_copy(w_out.at[:, my_columns], w_mine, load_sem.at[9]))
+    loads.append(pltpu.make_async_copy(chosen_hbm, chosen, load_sem.at[10]))
     for copy in loads:
         copy.start()
 
     barrier = pltpu.get_barrier_semaphore()
-    for device in (partner, across, beside, z_next, z_prev, y_next, y_prev):
+    greeted = (partner, across, beside) + toward_z[0] + toward_z[1] + toward_y[0] + toward_y[1]
+    for device in greeted:
         pl.semaphore_signal(barrier, inc=1, device_id=device, device_id_type=MESH)
-    pl.semaphore_wait(barrier, 7)
+    pl.semaphore_wait(barrier, len(greeted))
 
     def part(block, p):
         return kv.at[block, THIRD * p : THIRD * (p + 1), :]
@@ -138,13 +143,16 @@
         return plane * 4 + (1 - color) * 2 + core
 
     def z_copy(d, hop, p):
-        return send(mine(plane_of(d, hop - 1)), p, z_send.at[d, hop - 1, p], z_recv.at[d, hop - 1, p], toward_z[d])
+        source, stride = ((0, 1), (0, 2), (2, 1), (2, 2))[hop - 1]
+        return send(
+            mine(plane_of(d, source)), p, z_send.at[d, hop - 1, p], z_recv.at[d, hop - 1, p], toward_z[stride - 1][d]
+        )
 
     def y_copy(d, hop, p):
-        return send(mine(plane_of(d, hop)), p, y_send.at[d, hop - 1, p], y_recv.at[d, hop - 1, p], toward_y[d])
+        return send(mine(plane_of(d, hop)), p, y_send.at[d, hop - 1, p], y_recv.at[d, hop - 1, p], toward_y[0][d])
 
     def y_arrival(d, hop, p):
-        return send(other(plane_of(d, hop)), p, y_send.at[d, hop - 1, p], y_recv.at[d, hop - 1, p], toward_y[d])
+        return send(other(plane_of(d, hop)), p, y_send.at[d, hop - 1, p], y_recv.at[d, hop - 1, p], toward_y[0][d])
 
     def zp_copy(d, hop, p):
         return send(mine(plane_of(d, hop)), p, zp_send.at[d, hop - 1, p], zp_recv.at[d, hop - 1, p], partner)
@@ -168,9 +176,10 @@
 
     @pl.when(xh == color)
     def _():
-        for p in range(PIECES):
-            for d in range(2):
-                z_copy(d, 1, p).start()
+        for hop in (2, 1):
+            for p in range(PIECES):
+                for d in range(2):
+                    z_copy(d, hop, p).start()
 
     def w_rows(which, of_core):
         return pl.ds(pl.multiple_of((2 * of_core + which) * quarter, quarter), quarter)
@@ -200,6 +209,7 @@
     for copy in w_copies:
         copy.start()
 
+    loads[10].wait()
     block_ids = lax.broadcasted_iota(jnp.int32, (planes * 4, BLOCK), 0)
     listed = block_ids < 0
     for j in range(chosen.shape[1]):
@@ -217,6 +227,12 @@
         @pl.when(xh != color)
         def _():
             for d in range(2):
+                z_copy(d, 2, p).start()
+
+    @pl.when(xh != color)
+    def _():
+        for p in range(PIECES):
+            for d in range(2):
                 z_copy(d, 1, p).start()
 
     for copy in loads[5:8]:
@@ -231,8 +247,8 @@
     scale = (QK_NOPE + ROPE) ** -0.5 * math.log2(math.e)
     half = heads * BLOCK // 2
 
-    def attend(plane, r, own):
-        rows = slice(half * r, half * (r + 1))
+    def attend(plane, r, own=False):
+        rows = pl.ds(r * half, half)
         first = plane * 4
         keys = jnp.concatenate([kv[first + i, 0:BLOCK, :] for i in range(4)], axis=0)
         rotary = jnp.concatenate(
@@ -273,104 +289,108 @@
             columns = slice(128 * j, 128 * (j + 1))
             w_turned[which, columns, :] = source[:, columns].T
 
+    def attend_plane(plane, own=False):
+        def turn_of(r, c):
+            attend(plane, pl.multiple_of(r, 1), own)
+            return c
+
+        lax.fori_loop(0, 2, turn_of, 0)
+
+    def z_take(d, hop, p):
+        if carried(d, hop, p):
+            z_copy(d, hop, p).wait_recv()
+            if hop == 2:
+                z_copy(d, 3, p).start()
+                if carried(d, 4, p):
+                    z_copy(d, 4, p).start()
+            y_copy(d, hop, p).start()
+            zp_copy(d, hop, p).start()
+
+    def y_take(d, hop, p):
+        if carried(d, hop, p):
+            y_arrival(d, hop, p).wait_recv()
+            yp_copy(d, hop, p).start()
+
+    def complete(d, hop):
+        for p in range(PIECES):
+            if carried(d, hop, p):
+                zp_copy(d, hop, p).wait_recv()
+                yp_copy(d, hop, p).wait_recv()
+
+    def visit(d, hop):
+        complete(d, hop)
+        attend_plane(plane_of(d, hop))
+
+    both = range(2)
+    for d in both:
+        z_take(d, 2, 0)
     own_copy.wait_recv()
     for p in range(PIECES):
         xp_copies[p].wait_recv()
-
-    def step(hop, c):
-        for p in range(PIECES):
-            for d in range(2):
-
-                @pl.when((hop < 4) | ((hop == 4) & (p < 2 if d == 0 else p == 2)))
-                def _():
-                    z_copy(d, hop, p).wait_recv()
-
-                @pl.when((hop < 3) | ((hop == 3) & (p < 2 if d == 0 else p == 2)))
-                def _():
-                    z_copy(d, hop + 1, p).start()
-
-                @pl.when((hop < 4) | ((hop == 4) & (p < 2 if d == 0 else p == 2)))
-                def _():
-                    y_copy(d, hop, p).start()
-                    zp_copy(d, hop, p).start()
-
-            before = hop - 1
-            for d in range(2):
-
-                @pl.when((before >= 1) & ((before < 4) | ((before == 4) & (p < 2 if d == 0 else p == 2))))
-                def _():
-                    y_arrival(d, before, p).wait_recv()
-                    yp_copy(d, before, p).start()
-
-            if p == 0:
-
-                @pl.when(hop == 1)
-                def _():
-                    for r in range(2):
-                        attend(z, r, True)
-
-            if p == 2:
-
-                @pl.when(hop == 1)
-                def _():
-                    loads[9].wait()
-                    turn(w_mine, 0)
-
-                @pl.when(hop == 4)
-                def _():
-                    for copy in w_copies:
-                        copy.wait_recv()
-                    for copy in wp_copies:
-                        copy.start()
-
-                @pl.when(hop == 5)
-                def _():
-                    for copy in wp_copies:
-                        copy.wait_recv()
-                    turn(w_peer, 1)
-
-            ready = hop - 2
-            if p > 0:
-                d = p - 1
-
-                @pl.when((ready >= 1) & (ready < 4))
-                def _():
-                    for q in range(PIECES):
-                        zp_copy(d, ready, q).wait_recv()
-                        yp_copy(d, ready, q).wait_recv()
-                    for r in range(2):
-                        attend(plane_of(d, ready), r, False)
-
-        return c
-
-    lax.fori_loop(1, 6, step, 0)
-    for d in range(2):
-        for p in range(PIECES):
-            if carried(d, 4, p):
-                zp_copy(d, 4, p).wait_recv()
-                yp_copy(d, 4, p).wait_recv()
-    for r in range(2):
-        attend(plane_of(0, 4), r, False)
+    attend_plane(z, True)
+    for p in (1, 2):
+        for d in both:
+            z_take(d, 2, p)
+    loads[9].wait()
+    turn(w_mine, 0)
+    for p in range(PIECES):
+        for d in both:
+            z_take(d, 1, p)
+        for d in both:
+            y_take(d, 2, p)
+    for copy in w_copies:
+        copy.wait_recv()
+    for copy in wp_copies:
+        copy.start()
+    for p in range(PIECES):
+        for d in both:
+            z_take(d, 3, p)
+        for d in both:
+            z_take(d, 4, p)
+        for d in both:
+            y_take(d, 1, p)
+        if p == 0:
+            visit(0, 2)
+        if p == 1:
+            visit(1, 2)
+    visit(0, 1)
+    for p in range(PIECES):
+        for d in both:
+            y_take(d, 3, p)
+        for d in both:
+            y_take(d, 4, p)
+        if p == 0:
+            visit(1, 1)
+        if p == 1:
+            for copy in wp_copies:
+                copy.wait_recv()
+            turn(w_peer, 1)
+    visit(0, 3)
+    visit(1, 3)
+    for d in both:
+        complete(d, 4)
 
     loads[8].wait()
     v_copies = []
-    for h in range(heads):
-        rows = slice(BLOCK * h, BLOCK * (h + 1))
-        columns = slice(VHEAD * h, VHEAD * (h + 1))
-        denominator = jnp.sum(row_sum[rows, :], axis=1, keepdims=True)
-        mix = (acc[rows, :] / denominator).astype(jnp.bfloat16)
-        values[:, columns] = jnp.dot(mix, wuv_buf[h], preferred_element_type=jnp.float32).astype(jnp.bfloat16)
-        v_copies.append(
-            pltpu.make_async_remote_copy(
-                values.at[:, columns],
-                v_peer.at[:, columns],
-                v_send.at[h],
-                v_recv.at[h],
-                device_id=beside,
-                device_id_type=MESH,
+    for r in range(2):
+        attend(plane_of(0, 4), r)
+        for h in range(heads // 2 * r, heads // 2 * (r + 1)):
+            rows = slice(BLOCK * h, BLOCK * (h + 1))
+            columns = slice(VHEAD * h, VHEAD * (h + 1))
+            denominator = jnp.sum(row_sum[rows, :], axis=1, keepdims=True)
+            mix = (acc[rows, :] / denominator).astype(jnp.bfloat16)
+            values[:, columns] = jnp.dot(mix, wuv_buf[h], preferred_element_type=jnp.float32).astype(jnp.bfloat16)
+            v_copies.append(
+                pltpu.make_async_remote_copy(
+                    values.at[:, columns],
+                    v_peer.at[:, columns],
+                    v_send.at[h],
+                    v_recv.at[h],
+                    device_id=beside,
+                    device_id_type=MESH,
+                )
             )
-        )
-        v_copies[h].start()
+            v_copies[h].start()
 
     def owner(step):
         return lax.rem(y + step + 2 * ys, ys)
@@ -390,64 +410,67 @@
     def peer_part(step):
         piece[owner(step)] += product(step, 1, v_peer)
 
-    steps = [4, 3, -3, 2, -2, 1, -1, 0]
-    for step_at in steps:
-        own_part(step_at)
+    steps = [4, 3, -3, 1, -1, 2, -2, 0]
+    for away in steps:
+        own_part(away)
     for copy in v_copies:
         copy.wait_recv()
 
     rows_half = piece.shape[1] // 2
-
-    def hops_of(d, t):
-        return 4 if (d == 0) == (t == 0) else 3
-
-    def r_copy(d, t, k):
+    sign = (1, -1)
+
+    def r_copy(d, away, t):
+        slot = {4: 0, 3: 1 + t, 1: 3 + t, 2: 5 + t}[away]
+        stride = {4: 2, 3: 1, 1: 1, 2: 2}[away]
         return pltpu.make_async_remote_copy(
-            staged.at[d, t, k - 1],
-            landed.at[d, t, k - 1],
-            r_send.at[d, t, k - 1],
-            r_recv.at[d, t, k - 1],
-            device_id=toward_y[d],
+            staged.at[d, slot],
+            landed.at[d, slot],
+            r_send.at[d, slot],
+            r_recv.at[d, slot],
+            device_id=toward_y[stride - 1][d],
             device_id_type=MESH,
         )
 
-    def my_rows(step, t):
-        return piece[owner(step), rows_half * t : rows_half * (t + 1), :]
-
-    def send_sum(d, t, k):
-        away = hops_of(d, t) - k + 1
-        total = my_rows(away if d == 0 else -away, t)
-        if k > 1:
-            r_copy(d, t, k - 1).wait_recv()
-            total = total + landed[d, t, k - 2].astype(jnp.float32)
-        staged[d, t, k - 1] = total.astype(jnp.bfloat16)
-        r_copy(d, t, k).start()
-
-    chains = [(0, 0), (1, 1), (0, 1), (1, 0)]
+    def take_sum(d, away, t):
+        r_copy(d, away, t).wait_recv()
+        return landed[d, {4: 0, 3: 1 + t, 1: 3 + t, 2: 5 + t}[away]].astype(jnp.float32)
+
+    def send_sum(d, away, t):
+        total = piece[owner(sign[d] * away), rows_half * t : rows_half * (t + 1), :]
+        if away == 2:
+            total = total + take_sum(d, 3, t)
+            if t == d:
+                total = total + take_sum(d, 4, t)
+        staged[d, {4: 0, 3: 1 + t, 1: 3 + t, 2: 5 + t}[away]] = total.astype(jnp.bfloat16)
+        r_copy(d, away, t).start()
+
     peer_part(4)
-    send_sum(0, 0, 1)
-    send_sum(1, 1, 1)
-    peer_part(3)
-    send_sum(0, 1, 1)
-    peer_part(-3)
-    send_sum(1, 0, 1)
-    for step_at in (2, -2, 1, -1, 0):
-        peer_part(step_at)
-    for k in range(2, 5):
-        for d, t in chains:
-            if k <= hops_of(d, t):
-                send_sum(d, t, k)
-    for t in (1, 0):
-        total = my_rows(0, t)
-        for d in range(2):
-            n = hops_of(d, t)
-            r_copy(d, t, n).wait_recv()
-            total = total + landed[d, t, n - 1].astype(jnp.float32)
-        out[rows_half * t : rows_half * (t + 1), :] = total.astype(jnp.bfloat16)
-
-    for d, t in chains:
-        for k in range(1, hops_of(d, t) + 1):
-            r_copy(d, t, k).wait_send()
+    for d in both:
+        send_sum(d, 4, d)
+    for away in (3, 1):
+        for d in both:
+            peer_part(sign[d] * away)
+            for t in (d, 1 - d):
+                send_sum(d, away, t)
+    for away in (2, -2, 0):
+        peer_part(away)
+    for i in range(2):
+        for d in both:
+            send_sum(d, 2, (1 - d, d)[i])
+    mine_of = [piece[owner(0), rows_half * t : rows_half * (t + 1), :] for t in range(2)]
+    for t in range(2):
+        for d in both:
+            mine_of[t] = mine_of[t] + take_sum(d, 1, t)
+    for t in range(2):
+        for d in both:
+            mine_of[t] = mine_of[t] + take_sum(d, 2, t)
+        out[rows_half * t : rows_half * (t + 1), :] = mine_of[t].astype(jnp.bfloat16)
+
+    for d in both:
+        r_copy(d, 4, d).wait_send()
+        for away in (3, 1, 2):
+            for t in range(2):
+                r_copy(d, away, t).wait_send()
     for copy in w_copies + wp_copies + v_copies:
         copy.wait_send()
     for copy in x_copies + xp_copies + [own_copy]:
@@ -482,16 +505,7 @@
         return pl.pallas_call(
             kernel,
             out_shape=jax.ShapeDtypeStruct((cut, tokens), jnp.bfloat16),
-            in_specs=[
-                anywhere,
-                anywhere,
-                anywhere,
-                anywhere,
-                pl.BlockSpec(memory_space=pltpu.SMEM),
-                anywhere,
-                anywhere,
-                anywhere,
-            ],
+            in_specs=[anywhere] * 8,
             out_specs=pl.BlockSpec(memory_space=pltpu.VMEM),
             scratch_shapes=[
                 pltpu.VMEM((planes * 4, ROWS, LAT), jnp.bfloat16),
@@ -505,7 +519,7 @@
                 pltpu.VMEM((rows, 128), jnp.float32),
                 pltpu.VMEM((rows, 128), jnp.float32),
                 pltpu.VMEM((rows, LAT), jnp.float32),
-                dma((10,)),
+                dma((11,)),
                 dma((3,)),
                 dma((3,)),
                 dma((1,)),
@@ -521,14 +535,15 @@
                 pltpu.VMEM((tokens, depth), jnp.bfloat16),
                 pltpu.VMEM((tokens, depth), jnp.bfloat16),
                 pltpu.VMEM((ys, cut, tokens), jnp.float32),
-                pltpu.VMEM((2, 2, 4, cut // 2, tokens), jnp.bfloat16),
-                pltpu.VMEM((2, 2, 4, cut // 2, tokens), jnp.bfloat16),
+                pltpu.VMEM((2, 7, cut // 2, tokens), jnp.bfloat16),
+                pltpu.VMEM((2, 7, cut // 2, tokens), jnp.bfloat16),
                 dma((4,)),
                 dma((4,)),
                 dma((heads,)),
                 dma((heads,)),
-                dma((2, 2, 4)),
-                dma((2, 2, 4)),
+                dma((2, 7)),
+                dma((2, 7)),
+                pltpu.SMEM(chosen.shape, jnp.int32),
             ],
             compiler_params=pltpu.CompilerParams(
                 collective_id=0, has_side_effects=True, vmem_limit_bytes=67043328

time: 63.3 us -> 62.8 us (level)
  the two profiles are of different devices: /device:TPU:10 before, /device:TPU:2 now
where the time goes in v3:
time: 62.8 us; the launch traced here: 62.7 us
  Pallas kernels  61.2 us (97%)
  local copies, waits for them, and re-layouts  1.45 us (2%)
    pallas_call x1, Pallas kernels, on_device(): pl.pallas_call(kernel, out_shape=jax.ShapeDtypeStruct((cut, tokens), jnp....  61.2 us
    unnamed x1, local copies, waits for them, and re-layouts  1.45 us

profile of v3, /device:TPU:2, one launch (start us, length us, event | category | flops | bytes accessed | tf_op | source)
XLA Modules:
  0.0 62.7 jit_solution(2754348665618193068)
XLA Ops:
  0.0 61.2 %shard_map.82 = bf16[224,128]{1,0:T(8,128)(2,1)} custom-call(bf16[128,512]{1,0:T(8,128)(2,1)} %refs_0_.1, bf16[128,256]{1,0:T(8,128)(2,1)} %refs_1_.1, bf16[1,128,512]{2,1,0:T(8,128)(2,1)} %refs_2_.1, bf16[1,64,128]{2,1,0:T(8,128)(2,1)} %refs_3_.1, s32[1,20]{1,0:T(1,128)} %refs_4_.1, bf16[4,128,512]{2,1,0:T(8,128)(2,1)} %refs_5_.1, ...), custom_call_target="tpu_custom_call" | custom-call | tf_op jit(solution)/shard_map/pallas_call | solution.py:505
  61.2 1.4 %copy.10 = bf16[128,224]{0,1:T(8,128)(2,1)} copy(bf16[128,224]{0,1:T(8,128)(2,1)} %bitcast.1) | data formatting | bytes 114688

commit v4 on v3

--- a/solution.py
+++ b/solution.py
@@ -143,7 +143,7 @@
         return plane * 4 + (1 - color) * 2 + core
 
     def z_copy(d, hop, p):
-        source, stride = ((0, 1), (0, 2), (2, 1), (2, 2))[hop - 1]
+        source, stride = ((0, 1), (1, 1), (2, 1), (2, 2))[hop - 1]
         return send(
             mine(plane_of(d, source)), p, z_send.at[d, hop - 1, p], z_recv.at[d, hop - 1, p], toward_z[stride - 1][d]
         )
@@ -176,10 +176,9 @@
 
     @pl.when(xh == color)
     def _():
-        for hop in (2, 1):
-            for p in range(PIECES):
-                for d in range(2):
-                    z_copy(d, hop, p).start()
+        for p in range(PIECES):
+            for d in range(2):
+                z_copy(d, 1, p).start()
 
     def w_rows(which, of_core):
         return pl.ds(pl.multiple_of((2 * of_core + which) * quarter, quarter), quarter)
@@ -227,12 +226,6 @@
         @pl.when(xh != color)
         def _():
             for d in range(2):
-                z_copy(d, 2, p).start()
-
-    @pl.when(xh != color)
-    def _():
-        for p in range(PIECES):
-            for d in range(2):
                 z_copy(d, 1, p).start()
 
     for copy in loads[5:8]:
@@ -247,16 +240,13 @@
     scale = (QK_NOPE + ROPE) ** -0.5 * math.log2(math.e)
     half = heads * BLOCK // 2
 
-    def attend(plane, r, own=False):
-        rows = pl.ds(r * half, half)
-        first = plane * 4
-        keys = jnp.concatenate([kv[first + i, 0:BLOCK, :] for i in range(4)], axis=0)
+    def attend(blocks, r, own=False):
+        rows = slice(r * half, (r + 1) * half)
+        keys = jnp.concatenate([kv[b, 0:BLOCK, :] for b in blocks], axis=0)
         rotary = jnp.concatenate(
             [
-                jnp.concatenate(
-                    [kv[first + i, BLOCK:ROWS, 128 * j : 128 * (j + 1)] for j in range(4)], axis=0
-                )
-                for i in range(4)
+                jnp.concatenate([kv[b, BLOCK:ROWS, 128 * j : 128 * (j + 1)] for j in range(4)], axis=0)
+                for b in blocks
             ],
             axis=1,
         )
@@ -264,7 +254,7 @@
             q_lat[rows, :], keys, (((1,), (1,)), ((), ())), preferred_element_type=jnp.float32
         )
         scores = scores + jnp.dot(q_rot[rows, :], rotary, preferred_element_type=jnp.float32)
-        hidden = jnp.concatenate([bias[pl.ds(first + i, 1), :] for i in range(4)], axis=1)
+        hidden = jnp.concatenate([bias[pl.ds(b, 1), :] for b in blocks], axis=1)
         scores = scores * scale + hidden
         if own:
             t_ids = lax.broadcasted_iota(jnp.int32, scores.shape, 0) % BLOCK
@@ -275,9 +265,9 @@
         old_max = row_max[rows, :]
         new_max = jnp.maximum(old_max, jnp.max(scores, axis=1, keepdims=True))
         factor = jnp.exp2(old_max - new_max)
-        wide = jnp.concatenate([new_max] * 4, axis=1)
+        wide = jnp.concatenate([new_max] * len(blocks), axis=1)
         exponent = jnp.exp2(scores - wide)
-        total = exponent[:, 0:128] + exponent[:, 128:256] + exponent[:, 256:384] + exponent[:, 384:512]
+        total = sum(exponent[:, 128 * i : 128 * (i + 1)] for i in range(1, len(blocks))) + exponent[:, 0:128]
         row_max[rows, :] = new_max
         row_sum[rows, :] = row_sum[rows, :] * factor + total
         acc[rows, :] = acc[rows, :] * jnp.concatenate([factor] * 4, axis=1) + jnp.dot(
@@ -289,91 +279,99 @@
             columns = slice(128 * j, 128 * (j + 1))
             w_turned[which, columns, :] = source[:, columns].T
 
-    def attend_plane(plane, own=False):
-        def turn_of(r, c):
-            attend(plane, pl.multiple_of(r, 1), own)
-            return c
-
-        lax.fori_loop(0, 2, turn_of, 0)
-
-    def z_take(d, hop, p):
-        if carried(d, hop, p):
-            z_copy(d, hop, p).wait_recv()
-            if hop == 2:
-                z_copy(d, 3, p).start()
-                if carried(d, 4, p):
-                    z_copy(d, 4, p).start()
-            y_copy(d, hop, p).start()
-            zp_copy(d, hop, p).start()
-
-    def y_take(d, hop, p):
-        if carried(d, hop, p):
-            y_arrival(d, hop, p).wait_recv()
-            yp_copy(d, hop, p).start()
-
-    def complete(d, hop):
-        for p in range(PIECES):
+    both = range(2)
+
+    def z_take(hop, p):
+        for d in both:
             if carried(d, hop, p):
-                zp_copy(d, hop, p).wait_recv()
-                yp_copy(d, hop, p).wait_recv()
-
-    def visit(d, hop):
-        complete(d, hop)
-        attend_plane(plane_of(d, hop))
-
-    both = range(2)
-    for d in both:
-        z_take(d, 2, 0)
+                z_copy(d, hop, p).wait_recv()
+                for later in {1: (2,), 2: (3, 4)}.get(hop, ()):
+                    if carried(d, later, p):
+                        z_copy(d, later, p).start()
+        for d in both:
+            if carried(d, hop, p):
+                y_copy(d, hop, p).start()
+                zp_copy(d, hop, p).start()
+
+    def y_take(hop, p):
+        for d in both:
+            if carried(d, hop, p):
+                y_arrival(d, hop, p).wait_recv()
+                yp_copy(d, hop, p).start()
+
+    def chunk(hop, by_z):
+        for d in both:
+            for p in range(PIECES):
+                if carried(d, hop, p):
+                    (zp_copy if by_z else yp_copy)(d, hop, p).wait_recv()
+        which = color if by_z else 1 - color
+        firsts = [plane_of(d, hop) * 4 + which * 2 for d in both[: 1 if hop == 4 else 2]]
+        return [first + i for first in firsts for i in range(2)]
+
+    z_take(1, 0)
     own_copy.wait_recv()
     for p in range(PIECES):
         xp_copies[p].wait_recv()
-    attend_plane(z, True)
-    for p in (1, 2):
-        for d in both:
-            z_take(d, 2, p)
+    own_plane = [z * 4 + i for i in range(4)]
+    attend(own_plane, 0, True)
+    z_take(1, 1)
+    attend(own_plane, 1, True)
+    z_take(1, 2)
+    blocks = chunk(1, True)
+    attend(blocks, 0)
+    z_take(2, 0)
+    y_take(1, 0)
+    attend(blocks, 1)
+    z_take(2, 1)
+    y_take(1, 1)
     loads[9].wait()
     turn(w_mine, 0)
-    for p in range(PIECES):
-        for d in both:
-            z_take(d, 1, p)
-        for d in both:
-            y_take(d, 2, p)
+    z_take(2, 2)
+    y_take(1, 2)
+    blocks = chunk(2, True)
+    attend(blocks, 0)
+    z_take(3, 0)
+    y_take(2, 0)
+    attend(blocks, 1)
     for copy in w_copies:
         copy.wait_recv()
     for copy in wp_copies:
         copy.start()
+    z_take(3, 1)
+    y_take(2, 1)
+    blocks = chunk(1, False)
+    attend(blocks, 0)
+    z_take(3, 2)
+    y_take(2, 2)
+    attend(blocks, 1)
     for p in range(PIECES):
-        for d in both:
-            z_take(d, 3, p)
-        for d in both:
-            z_take(d, 4, p)
-        for d in both:
-            y_take(d, 1, p)
-        if p == 0:
-            visit(0, 2)
-        if p == 1:
-            visit(1, 2)
-    visit(0, 1)
+        z_take(4, p)
+    for copy in wp_copies:
+        copy.wait_recv()
+    turn(w_peer, 1)
+    blocks = chunk(2, False)
+    attend(blocks, 0)
+    y_take(3, 0)
+    attend(blocks, 1)
+    y_take(3, 1)
+    blocks = chunk(3, True)
+    attend(blocks, 0)
+    y_take(3, 2)
+    attend(blocks, 1)
     for p in range(PIECES):
-        for d in both:
-            y_take(d, 3, p)
-        for d in both:
-            y_take(d, 4, p)
-        if p == 0:
-            visit(1, 1)
-        if p == 1:
-            for copy in wp_copies:
-                copy.wait_recv()
-            turn(w_peer, 1)
-    visit(0, 3)
-    visit(1, 3)
-    for d in both:
-        complete(d, 4)
+        y_take(4, p)
+    blocks = chunk(4, True)
+    attend(blocks, 0)
+    attend(blocks, 1)
+    blocks = chunk(3, False)
+    attend(blocks, 0)
+    attend(blocks, 1)
+    blocks = chunk(4, False)
 
     loads[8].wait()
     v_copies = []
     for r in range(2):
-        attend(plane_of(0, 4), r)
+        attend(blocks, r)
         for h in range(heads // 2 * r, heads // 2 * (r + 1)):
             rows = slice(BLOCK * h, BLOCK * (h + 1))
             columns = slice(VHEAD * h, VHEAD * (h + 1))

time: 62.8 us -> 61.1 us (0.973)
  the two profiles are of different devices: /device:TPU:2 before, /device:TPU:10 now
where the time goes in v4:
time: 61.1 us; the launch traced here: 61 us
  Pallas kernels  59.5 us (97%)
  local copies, waits for them, and re-layouts  1.45 us (2%)
    pallas_call x1, Pallas kernels, on_device(): pl.pallas_call(kernel, out_shape=jax.ShapeDtypeStruct((cut, tokens), jnp....  59.5 us
    unnamed x1, local copies, waits for them, and re-layouts  1.45 us

profile of v4, /device:TPU:10, one launch (start us, length us, event | category | flops | bytes accessed | tf_op | source)
XLA Modules:
  0.0 61.0 jit_solution(15228695024441501442)
XLA Ops:
  0.0 59.5 %shard_map.82 = bf16[224,128]{1,0:T(8,128)(2,1)} custom-call(bf16[128,512]{1,0:T(8,128)(2,1)} %refs_0_.1, bf16[128,256]{1,0:T(8,128)(2,1)} %refs_1_.1, bf16[1,128,512]{2,1,0:T(8,128)(2,1)} %refs_2_.1, bf16[1,64,128]{2,1,0:T(8,128)(2,1)} %refs_3_.1, s32[1,20]{1,0:T(1,128)} %refs_4_.1, bf16[4,128,512]{2,1,0:T(8,128)(2,1)} %refs_5_.1, ...), custom_call_target="tpu_custom_call" | custom-call | tf_op jit(solution)/shard_map/pallas_call | solution.py:503
  59.5 1.4 %copy.10 = bf16[128,224]{0,1:T(8,128)(2,1)} copy(bf16[128,224]{0,1:T(8,128)(2,1)} %bitcast.1) | data formatting | bytes 114688

commit v5 on v4

--- a/solution.py
+++ b/solution.py
@@ -91,9 +91,9 @@
     beside = (ci, (1 - xl) * ys + y)
     z_next, z_prev = (ctx_at(z + 1), hi), (ctx_at(z - 1), hi)
     y_next, y_prev = (ci, head_at(y + 1)), (ci, head_at(y - 1))
-    z_over, z_under = (ctx_at(z + 2), hi), (ctx_at(z - 2), hi)
     y_over, y_under = (ci, head_at(y + 2)), (ci, head_at(y - 2))
-    toward_z = ((z_next, z_prev), (z_over, z_under))
+    toward_z = (z_next, z_prev)
+    aslant = ((ctx_at(z + 1), head_at(y + 1)), (ctx_at(z - 1), head_at(y - 1)))
     toward_y = ((y_next, y_prev), (y_over, y_under))
 
     loads = [pltpu.make_async_copy(latent.at[0], kv.at[ci, 0:BLOCK, :], load_sem.at[0])]
@@ -120,7 +120,7 @@
         copy.start()
 
     barrier = pltpu.get_barrier_semaphore()
-    greeted = (partner, across, beside) + toward_z[0] + toward_z[1] + toward_y[0] + toward_y[1]
+    greeted = (partner, across, beside) + toward_z + aslant + toward_y[0] + toward_y[1]
     for device in greeted:
         pl.semaphore_signal(barrier, inc=1, device_id=device, device_id_type=MESH)
     pl.semaphore_wait(barrier, len(greeted))
@@ -143,12 +143,13 @@
         return plane * 4 + (1 - color) * 2 + core
 
     def z_copy(d, hop, p):
-        source, stride = ((0, 1), (1, 1), (2, 1), (2, 2))[hop - 1]
         return send(
-            mine(plane_of(d, source)), p, z_send.at[d, hop - 1, p], z_recv.at[d, hop - 1, p], toward_z[stride - 1][d]
+            mine(plane_of(d, hop - 1)), p, z_send.at[d, hop - 1, p], z_recv.at[d, hop - 1, p], toward_z[d]
         )
 
     def y_copy(d, hop, p):
+        if hop == 4:
+            return send(mine(plane_of(d, 3)), p, y_send.at[d, 3, p], y_recv.at[d, 3, p], aslant[d])
         return send(mine(plane_of(d, hop)), p, y_send.at[d, hop - 1, p], y_recv.at[d, hop - 1, p], toward_y[0][d])
 
     def y_arrival(d, hop, p):
@@ -241,7 +242,7 @@
     half = heads * BLOCK // 2
 
     def attend(blocks, r, own=False):
-        rows = slice(r * half, (r + 1) * half)
+        rows = slice(0, 2 * half) if r is None else slice(r * half, (r + 1) * half)
         keys = jnp.concatenate([kv[b, 0:BLOCK, :] for b in blocks], axis=0)
         rotary = jnp.concatenate(
             [
@@ -285,12 +286,15 @@
         for d in both:
             if carried(d, hop, p):
                 z_copy(d, hop, p).wait_recv()
-                for later in {1: (2,), 2: (3, 4)}.get(hop, ()):
+                for later in {1: (2,), 2: (3,), 3: (4,)}.get(hop, ()):
                     if carried(d, later, p):
                         z_copy(d, later, p).start()
+                        if later == 4:
+                            y_copy(d, 4, p).start()
         for d in both:
             if carried(d, hop, p):
-                y_copy(d, hop, p).start()
+                if hop < 4:
+                    y_copy(d, hop, p).start()
                 zp_copy(d, hop, p).start()
 
     def y_take(hop, p):
@@ -299,14 +303,16 @@
                 y_arrival(d, hop, p).wait_recv()
                 yp_copy(d, hop, p).start()
 
+    def complete(d, hop, by_z):
+        for p in range(PIECES):
+            if carried(d, hop, p):
+                (zp_copy if by_z else yp_copy)(d, hop, p).wait_recv()
+
     def chunk(hop, by_z):
-        for d in both:
-            for p in range(PIECES):
-                if carried(d, hop, p):
-                    (zp_copy if by_z else yp_copy)(d, hop, p).wait_recv()
         which = color if by_z else 1 - color
-        firsts = [plane_of(d, hop) * 4 + which * 2 for d in both[: 1 if hop == 4 else 2]]
-        return [first + i for first in firsts for i in range(2)]
+        for d in both:
+            complete(d, hop, by_z)
+        return [plane_of(d, hop) * 4 + which * 2 + i for d in both for i in range(2)]
 
     z_take(1, 0)
     own_copy.wait_recv()
@@ -344,29 +350,24 @@
     z_take(3, 2)
     y_take(2, 2)
     attend(blocks, 1)
-    for p in range(PIECES):
-        z_take(4, p)
     for copy in wp_copies:
         copy.wait_recv()
     turn(w_peer, 1)
     blocks = chunk(2, False)
-    attend(blocks, 0)
-    y_take(3, 0)
-    attend(blocks, 1)
-    y_take(3, 1)
+    attend(blocks, None)
+    for p in range(PIECES):
+        z_take(4, p)
+        y_take(3, p)
     blocks = chunk(3, True)
-    attend(blocks, 0)
-    y_take(3, 2)
-    attend(blocks, 1)
+    attend(blocks, None)
     for p in range(PIECES):
         y_take(4, p)
-    blocks = chunk(4, True)
-    attend(blocks, 0)
-    attend(blocks, 1)
     blocks = chunk(3, False)
-    attend(blocks, 0)
-    attend(blocks, 1)
-    blocks = chunk(4, False)
+    attend(blocks, None)
+    for d in both:
+        for by_z in (True, False):
+            complete(d, 4, by_z)
+    blocks = [plane_of(0, 4) * 4 + i for i in range(4)]
 
     loads[8].wait()
     v_copies = []

time: 61.1 us -> 57.8 us (0.946)
  the two profiles are of different devices: /device:TPU:10 before, /device:TPU:2 now
where the time goes in v5:
time: 57.8 us; the launch traced here: 57.7 us
  Pallas kernels  56.2 us (97%)
  local copies, waits for them, and re-layouts  1.45 us (3%)
    pallas_call x1, Pallas kernels, on_device(): pl.pallas_call(kernel, out_shape=jax.ShapeDtypeStruct((cut, tokens), jnp....  56.2 us
    unnamed x1, local copies, waits for them, and re-layouts  1.45 us

profile of v5, /device:TPU:2, one launch (start us, length us, event | category | flops | bytes accessed | tf_op | source)
XLA Modules:
  0.0 57.7 jit_solution(13053882348317558427)
XLA Ops:
  0.0 56.2 %shard_map.82 = bf16[224,128]{1,0:T(8,128)(2,1)} custom-call(bf16[128,512]{1,0:T(8,128)(2,1)} %refs_0_.1, bf16[128,256]{1,0:T(8,128)(2,1)} %refs_1_.1, bf16[1,128,512]{2,1,0:T(8,128)(2,1)} %refs_2_.1, bf16[1,64,128]{2,1,0:T(8,128)(2,1)} %refs_3_.1, s32[1,20]{1,0:T(1,128)} %refs_4_.1, bf16[4,128,512]{2,1,0:T(8,128)(2,1)} %refs_5_.1, ...), custom_call_target="tpu_custom_call" | custom-call | tf_op jit(solution)/shard_map/pallas_call | solution.py:504
  56.2 1.4 %copy.10 = bf16[128,224]{0,1:T(8,128)(2,1)} copy(bf16[128,224]{0,1:T(8,128)(2,1)} %bitcast.1) | data formatting | bytes 114688

commit v6 on v5

--- a/solution.py
+++ b/solution.py
@@ -96,6 +96,11 @@
     aslant = ((ctx_at(z + 1), head_at(y + 1)), (ctx_at(z - 1), head_at(y - 1)))
     toward_y = ((y_next, y_prev), (y_over, y_under))
 
+    barrier = pltpu.get_barrier_semaphore()
+    greeted = (partner, across, beside) + toward_z + aslant + toward_y[0] + toward_y[1]
+    for device in greeted:
+        pl.semaphore_signal(barrier, inc=1, device_id=device, device_id_type=MESH)
+
     loads = [pltpu.make_async_copy(latent.at[0], kv.at[ci, 0:BLOCK, :], load_sem.at[0])]
     for i in range(4):
         loads.append(
@@ -119,10 +124,6 @@
     for copy in loads:
         copy.start()
 
-    barrier = pltpu.get_barrier_semaphore()
-    greeted = (partner, across, beside) + toward_z + aslant + toward_y[0] + toward_y[1]
-    for device in greeted:
-        pl.semaphore_signal(barrier, inc=1, device_id=device, device_id_type=MESH)
     pl.semaphore_wait(barrier, len(greeted))
 
     def part(block, p):
@@ -456,20 +457,6 @@
     for i in range(2):
         for d in both:
             send_sum(d, 2, (1 - d, d)[i])
-    mine_of = [piece[owner(0), rows_half * t : rows_half * (t + 1), :] for t in range(2)]
-    for t in range(2):
-        for d in both:
-            mine_of[t] = mine_of[t] + take_sum(d, 1, t)
-    for t in range(2):
-        for d in both:
-            mine_of[t] = mine_of[t] + take_sum(d, 2, t)
-        out[rows_half * t : rows_half * (t + 1), :] = mine_of[t].astype(jnp.bfloat16)
-
-    for d in both:
-        r_copy(d, 4, d).wait_send()
-        for away in (3, 1, 2):
-            for t in range(2):
-                r_copy(d, away, t).wait_send()
     for copy in w_copies + wp_copies + v_copies:
         copy.wait_send()
     for copy in x_copies + xp_copies + [own_copy]:
@@ -482,6 +469,21 @@
                     y_copy(d, hop, p).wait_send()
                     zp_copy(d, hop, p).wait_send()
                     yp_copy(d, hop, p).wait_send()
+
+    mine_of = [piece[owner(0), rows_half * t : rows_half * (t + 1), :] for t in range(2)]
+    for t in range(2):
+        for d in both:
+            mine_of[t] = mine_of[t] + take_sum(d, 1, t)
+    for t in range(2):
+        for d in both:
+            mine_of[t] = mine_of[t] + take_sum(d, 2, t)
+        out[rows_half * t : rows_half * (t + 1), :] = mine_of[t].astype(jnp.bfloat16)
+
+    for d in both:
+        r_copy(d, 4, d).wait_send()
+        for away in (3, 1, 2):
+            for t in range(2):
+                r_copy(d, away, t).wait_send()
 
 
 def solution(mesh):

time: 57.8 us -> 57.6 us (level)
  the two profiles are of different devices: /device:TPU:2 before, /device:TPU:10 now
where the time goes in v6:
time: 57.6 us; the launch traced here: 57.5 us
  Pallas kernels  56 us (97%)
  local copies, waits for them, and re-layouts  1.45 us (3%)
    pallas_call x1, Pallas kernels, on_device(): pl.pallas_call(kernel, out_shape=jax.ShapeDtypeStruct((cut, tokens), jnp....  56 us
    unnamed x1, local copies, waits for them, and re-layouts  1.45 us

profile of v6, /device:TPU:10, one launch (start us, length us, event | category | flops | bytes accessed | tf_op | source)
XLA Modules:
  0.0 57.5 jit_solution(3572139396074126347)
XLA Ops:
  0.0 56.0 %shard_map.82 = bf16[224,128]{1,0:T(8,128)(2,1)} custom-call(bf16[128,512]{1,0:T(8,128)(2,1)} %refs_0_.1, bf16[128,256]{1,0:T(8,128)(2,1)} %refs_1_.1, bf16[1,128,512]{2,1,0:T(8,128)(2,1)} %refs_2_.1, bf16[1,64,128]{2,1,0:T(8,128)(2,1)} %refs_3_.1, s32[1,20]{1,0:T(1,128)} %refs_4_.1, bf16[4,128,512]{2,1,0:T(8,128)(2,1)} %refs_5_.1, ...), custom_call_target="tpu_custom_call" | custom-call | tf_op jit(solution)/shard_map/pallas_call | solution.py:506
  56.0 1.4 %copy.10 = bf16[128,224]{0,1:T(8,128)(2,1)} copy(bf16[128,224]{0,1:T(8,128)(2,1)} %bitcast.1) | data formatting | bytes 114688

commit v7 on v6

--- a/solution.py
+++ b/solution.py
@@ -223,12 +223,13 @@
     xp_copies = [send(across_block, p, xp_send.at[p], xp_recv.at[p], partner) for p in range(PIECES)]
     for p in range(PIECES):
         x_copies[p].wait_recv()
-        xp_copies[p].start()
 
         @pl.when(xh != color)
         def _():
             for d in range(2):
                 z_copy(d, 1, p).start()
+
+        xp_copies[p].start()
 
     for copy in loads[5:8]:
         copy.wait()

time: 57.6 us -> 57.6 us (level)
  no operation moved by 1% of the time
where the time goes in v7:
time: 57.6 us; the launch traced here: 57.5 us
  Pallas kernels  56 us (97%)
  local copies, waits for them, and re-layouts  1.45 us (3%)
    pallas_call x1, Pallas kernels, on_device(): pl.pallas_call(kernel, out_shape=jax.ShapeDtypeStruct((cut, tokens), jnp....  56 us
    unnamed x1, local copies, waits for them, and re-layouts  1.45 us

profile of v7, /device:TPU:10, one launch (start us, length us, event | category | flops | bytes accessed | tf_op | source)
XLA Modules:
  0.0 57.5 jit_solution(3772651647753730943)
XLA Ops:
  0.0 56.0 %shard_map.82 = bf16[224,128]{1,0:T(8,128)(2,1)} custom-call(bf16[128,512]{1,0:T(8,128)(2,1)} %refs_0_.1, bf16[128,256]{1,0:T(8,128)(2,1)} %refs_1_.1, bf16[1,128,512]{2,1,0:T(8,128)(2,1)} %refs_2_.1, bf16[1,64,128]{2,1,0:T(8,128)(2,1)} %refs_3_.1, s32[1,20]{1,0:T(1,128)} %refs_4_.1, bf16[4,128,512]{2,1,0:T(8,128)(2,1)} %refs_5_.1, ...), custom_call_target="tpu_custom_call" | custom-call | tf_op jit(solution)/shard_map/pallas_call | solution.py:507
  56.0 1.4 %copy.10 = bf16[128,224]{0,1:T(8,128)(2,1)} copy(bf16[128,224]{0,1:T(8,128)(2,1)} %bitcast.1) | data formatting | bytes 114688
